TPU v7x, 128 devices: a whole 4x4x4 slice. The times are simulated.
128 devices in a mesh: tm: 16 (over y, x), orb: 8 (over z, core).
Axes of the slice: x: 4, y: 4, z: 4, core: 2. Of those that a mesh axis runs over, the one named last changes fastest.
Arguments:
- forward: bfloat16 [2, 2, 512, 128, 128], P(None, None, 'tm'), may hold values from -2 to 2
- backward_slab: bfloat16 [2, 2, 512, 128, 128], P(None, None, 'tm', 'orb'), may hold values from -2 to 2
- slot_time: int32 [512], replicated, may hold values from 0 to 511, as said below
- pattern: int32 [128, 128], replicated, may hold values 0 or 1
- coupling: float32 [128, 128], replicated, may hold values from -1 to 1
- hamiltonian: float32 [128, 128], replicated, may hold values from -0.8 to 0.8
- lesser_now: float32 [2, 128, 128], replicated, may hold values from -1.5 to 1.5
Outputs:
- lesser_next: float32 [2, 128, 128], P(None, 'orb')
Inputs may be any that keep to these rules, and one draw needn't show every extreme that they name: slot_time is a permutation of the 512 history times. The 32 slots of each index d of tm hold exactly 32 // 16 times of the range [e * 32, (e + 1) * 32) for every index e of tm.
All inputs are finite; a program needn't handle non-finite values.
Results may differ from a plain program's by a relative error of at most 0.0054.
Values may be sent and summed in bfloat16 or wider, within the bound.
No kernel may reach another device: no remote copies, remote signals or barrier semaphores. Data moves between devices by JAX's collectives and lax.ppermute only.
A program may use at most 64 MiB of HBM per device.

v0:
```python
import math
import jax
import jax.numpy as jnp
from jax import lax
from jax.sharding import PartitionSpec as P

history_step = 0.02
update_step = 0.5


def complex_einsum(form, left_re, left_im, right_re, right_im):
    real_part = jnp.einsum(
        form, left_re, right_re, preferred_element_type=jnp.float32
    ) - jnp.einsum(form, left_im, right_im, preferred_element_type=jnp.float32)
    imag_part = jnp.einsum(
        form, left_re, right_im, preferred_element_type=jnp.float32
    ) + jnp.einsum(form, left_im, right_re, preferred_element_type=jnp.float32)
    return (real_part, imag_part)


def self_energy(fwd_re, fwd_im, back_re, back_im, interaction, inter_rows, row_start, row_count):
    rows_re = lax.dynamic_slice_in_dim(fwd_re, row_start, row_count, 1)
    rows_im = lax.dynamic_slice_in_dim(fwd_im, row_start, row_count, 1)
    fwd_re32 = fwd_re.astype(jnp.float32)
    fwd_im32 = fwd_im.astype(jnp.float32)
    trans_re = jnp.swapaxes(back_re, 1, 2).astype(jnp.float32)
    trans_im = jnp.swapaxes(back_im, 1, 2).astype(jnp.float32)
    bubble_re = (fwd_re32 * trans_re - fwd_im32 * trans_im).astype(jnp.bfloat16)
    bubble_im = (fwd_re32 * trans_im + fwd_im32 * trans_re).astype(jnp.bfloat16)
    left_re = jnp.einsum(
        "ik,skj->sij", inter_rows, bubble_re, preferred_element_type=jnp.float32
    ).astype(jnp.bfloat16)
    left_im = jnp.einsum(
        "ik,skj->sij", inter_rows, bubble_im, preferred_element_type=jnp.float32
    ).astype(jnp.bfloat16)
    screen_re = jnp.einsum("sik,kj->sij", left_re, interaction, preferred_element_type=jnp.float32)
    screen_im = jnp.einsum("sik,kj->sij", left_im, interaction, preferred_element_type=jnp.float32)
    rows_re32 = rows_re.astype(jnp.float32)
    rows_im32 = rows_im.astype(jnp.float32)
    direct_re = rows_re32 * screen_re - rows_im32 * screen_im
    direct_im = rows_re32 * screen_im + rows_im32 * screen_re
    inter_rows32 = inter_rows.astype(jnp.float32)
    scaled_re = (inter_rows32[None, :, :, None] * fwd_re32[:, None]).astype(jnp.bfloat16)
    scaled_im = (inter_rows32[None, :, :, None] * fwd_im32[:, None]).astype(jnp.bfloat16)
    inner_re, inner_im = complex_einsum("slm,simj->silj", back_re, back_im, scaled_re, scaled_im)
    inter32 = interaction.astype(jnp.float32)
    weighted_re = (inner_re * inter32).astype(jnp.bfloat16)
    weighted_im = (inner_im * inter32).astype(jnp.bfloat16)
    exch_re, exch_im = complex_einsum("sil,silj->sij", rows_re, rows_im, weighted_re, weighted_im)
    sigma_re = (direct_re - exch_re).astype(jnp.bfloat16)
    sigma_im = (direct_im - exch_im).astype(jnp.bfloat16)
    return (sigma_re, sigma_im)


def block_terms(fwd_block, back_block, weights, interaction, inter_rows, row_start, row_count):
    summed = None
    scale = weights[:, None, None]
    for branch in (0, 1):
        other = 1 - branch
        factor = 1.0 if branch == 0 else -1.0
        sigma_re, sigma_im = self_energy(
            fwd_block[branch, 0],
            fwd_block[branch, 1],
            back_block[other, 0],
            back_block[other, 1],
            interaction,
            inter_rows,
            row_start,
            row_count,
        )
        prod_re, prod_im = complex_einsum(
            "sil,slj->sij", sigma_re, sigma_im, back_block[other, 0], back_block[other, 1]
        )
        term = factor * jnp.stack(
            [jnp.sum(scale * prod_re, axis=0), jnp.sum(scale * prod_im, axis=0)]
        )
        summed = term if summed is None else summed + term
    return summed


def history_terms(fwd_part, back_part, weights, interaction, inter_rows, row_start, row_count):
    slices_here = fwd_part.shape[2]
    block_size = math.gcd(max(4, 128 // row_count), slices_here)
    block_count = slices_here // block_size
    orbitals = fwd_part.shape[3]

    def add_block(block, running):
        start = block * block_size
        fwd_block = lax.dynamic_slice_in_dim(fwd_part, start, block_size, 2)
        back_block = lax.dynamic_slice_in_dim(back_part, start, block_size, 2)
        weight_block = lax.dynamic_slice_in_dim(weights, start, block_size, 0)
        return running + block_terms(
            fwd_block, back_block, weight_block, interaction, inter_rows, row_start, row_count
        )

    initial = jnp.zeros((2, row_count, orbitals), jnp.float32)
    return lax.fori_loop(0, block_count, add_block, initial)


def on_device(forward, backward_slab, slot_time, pattern, coupling, hamiltonian, lesser_now):
    tm_count = lax.axis_size("tm")
    my_time = lax.axis_index("tm")
    my_orb = lax.axis_index("orb")
    per_device = forward.shape[2]
    row_count = backward_slab.shape[3]
    per_peer = per_device // tm_count
    slices_all = per_device * tm_count
    row_start = my_orb * row_count
    time_start = my_time * per_device
    holder_of = slot_time // per_device
    my_holders = lax.dynamic_slice_in_dim(holder_of, time_start, per_device)
    send_order = jnp.argsort(my_holders, stable=True)
    sorted_slab = jnp.take(backward_slab, send_order, axis=2)
    holder_grid = holder_of.reshape(tm_count, per_device)
    time_grid = slot_time.reshape(tm_count, per_device)
    not_mine = (holder_grid != my_time).astype(jnp.int32)
    positions = jnp.argsort(not_mine, axis=1, stable=True)[:, :per_peer]
    times_here = jnp.take_along_axis(time_grid, positions, axis=1).reshape(per_device)
    natural = jnp.argsort(times_here - time_start)
    masked = coupling * pattern.astype(jnp.float32)
    interaction = ((masked + masked.T) * 0.5).astype(jnp.bfloat16)
    inter_rows = lax.dynamic_slice_in_dim(interaction, row_start, row_count, 0)
    time_index = time_start + jnp.arange(per_device, dtype=jnp.int32)
    edges = (time_index == 0) | (time_index == slices_all - 1)
    weights = jnp.where(edges, jnp.float32(0.5), jnp.float32(1.0)) * history_step
    full_sorted = lax.all_gather(sorted_slab, "orb", axis=3, tiled=True)
    arrived = lax.all_to_all(full_sorted, "tm", split_axis=2, concat_axis=2, tiled=True)
    back_full = jnp.take(arrived, natural, axis=2)
    local_collision = history_terms(
        forward, back_full, weights, interaction, inter_rows, row_start, row_count
    )
    summed_rows = lax.psum(local_collision, "tm")
    collision = lax.all_gather(summed_rows, "orb", axis=1, tiled=True)
    own_rows = lax.dynamic_slice_in_dim(collision, row_start, row_count, 1)
    own_columns = lax.dynamic_slice_in_dim(collision, row_start, row_count, 2)
    herm_re = own_rows[0] + own_columns[0].T
    herm_im = own_rows[1] - own_columns[1].T
    high = lax.Precision.HIGHEST
    ham_rows = lax.dynamic_slice_in_dim(hamiltonian, row_start, row_count, 0)
    lesser_rows = lax.dynamic_slice_in_dim(lesser_now, row_start, row_count, 1)
    comm_re = jnp.dot(ham_rows, lesser_now[0], precision=high) - jnp.dot(
        lesser_rows[0], hamiltonian, precision=high
    )
    comm_im = jnp.dot(ham_rows, lesser_now[1], precision=high) - jnp.dot(
        lesser_rows[1], hamiltonian, precision=high
    )
    next_re = lesser_rows[0] + update_step * (comm_im + herm_im)
    next_im = lesser_rows[1] - update_step * (comm_re + herm_re)
    return jnp.stack([next_re, next_im])


def solution(mesh):
    in_specs = (
        P(None, None, "tm", None, None),
        P(None, None, "tm", "orb", None),
        P(),
        P(),
        P(),
        P(),
        P(),
    )
    out_specs = P(None, "orb", None)
    return jax.shard_map(
        on_device, mesh=mesh, in_specs=in_specs, out_specs=out_specs, check_vma=False
    )
```

profile of v0, /device:TPU:1, one launch (start us, length us, event | category | flops | bytes accessed | tf_op | source)
XLA Modules:
  0.0 479.0 jit_solution(11907473625283810762)
XLA Ops:
  10.6 39.5 %all-gather.2.cloned.1.call-done = bf16[2,2,32,128,128]{4,3,1,0,2:T(8,128)(2,1)} async-done(((bf16[2,2,32,16,128]{4,3,1,0,2:T(8,128)(2,1)}), bf16[2,2,32,128,128]{4,3,1,0,2:T(8,128)(2,1)}) %all-gather.2.cloned.1.call-update) | async-done | bytes 4194320 | tf_op jit(solution)/shard_map/all_gather | solution.py:126
  50.1 6.6 %all-to-all-start = ((bf16[2,2,32,128,128]{4,3,1,0,2:T(8,128)(2,1)}), bf16[2,2,32,128,128]{4,3,1,0,2:T(8,128)(2,1)}, u32[]{:S(2)}, u32[]{:S(2)}) async-start(bf16[2,2,32,128,128]{4,3,1,0,2:T(8,128)(2,1)} %all-gather.2.cloned.1.call-done), calls=%async_computation | async-start | bytes 8388608 | tf_op jit(solution)/shard_map/all_to_all | solution.py:127
  64.0 55.6 %all-to-all-done = bf16[2,2,32,128,128]{4,3,1,0,2:T(8,128)(2,1)} async-done(((bf16[2,2,32,128,128]{4,3,1,0,2:T(8,128)(2,1)}), bf16[2,2,32,128,128]{4,3,1,0,2:T(8,128)(2,1)}, u32[]{:S(2)}, u32[]{:S(2)}) %all-to-all-start) | async-done | bytes 4194336 | tf_op jit(solution)/shard_map/all_to_all | solution.py:127
  119.6 4.7 copy.45
  124.3 5.2 %gather_fusion.1 = bf16[32,2,2,128,128]{4,3,2,1,0:T(8,128)(2,1)} fusion(bf16[2,2,32,128,128]{4,3,2,1,0:T(8,128)(2,1)} %copy.45, s32[1024]{0:T(1024)S(1)} %pad_clamp_fusion), kind=kCustom, calls=%fused_computation.1 | custom fusion | bytes 8388736 | tf_op jit(solution)/shard_map/jit(_take)/gather | solution.py:128
  129.5 4.6 select_bitcast_fusion
  134.1 249.0 %while.16 = (s32[]{:T(128)}, f32[2,16,128]{2,1,0:T(8,128)}, f32[32]{0:T(128)S(1)}, bf16[2,2,32,128,128]{4,3,2,1,0:T(8,128)(2,1)}, s32[]{:T(128)}, /*index=5*/bf1...) while((s32[]{:T(128)}, f32[2,16,128]{2,1,0:T(8,128)}, ...), condition=%wide.region_8.9_spmd.clone, body=%wide.region_3.8_spmd.clone.sunk | while | flops 4459808768 | bytes 142112496 | solution.py:97
  148.4 2.6 fusion.413
  151.0 2.3 fusion.415
  153.3 2.3 fusion.414
  155.6 2.2 fusion.409
  157.8 2.6 fusion.410
  160.4 2.3 fusion.416
  162.7 2.3 fusion.411
  170.9 2.2 fusion.426
  173.2 2.6 fusion.427
  175.8 2.3 fusion.429
  178.1 2.3 fusion.428
  180.3 2.2 fusion.423
  182.5 2.6 fusion.424
  185.2 2.3 fusion.430
  187.5 2.3 fusion.425
  210.6 2.6 fusion.413
  213.3 2.3 fusion.415
  215.5 2.3 fusion.414
  217.8 2.2 fusion.409
  220.0 2.6 fusion.410
  222.7 2.3 fusion.416
  224.9 2.3 fusion.411
  233.2 2.2 fusion.426
  235.4 2.6 fusion.427
  238.0 2.3 fusion.429
  240.3 2.3 fusion.428
  244.8 2.6 fusion.424
  247.4 2.3 fusion.430
  249.7 2.3 fusion.425
  272.9 2.6 fusion.413
  275.5 2.3 fusion.415
  277.8 2.3 fusion.414
  282.3 2.6 fusion.410
  284.9 2.3 fusion.416
  287.2 2.3 fusion.411
  295.4 2.2 fusion.426
  297.6 2.6 fusion.427
  300.3 2.3 fusion.429
  302.5 2.3 fusion.428
  307.0 2.6 fusion.424
  309.7 2.3 fusion.430
  311.9 2.3 fusion.425
  335.1 2.6 fusion.413
  337.8 2.3 fusion.415
  340.0 2.3 fusion.414
  344.5 2.6 fusion.410
  347.2 2.3 fusion.416
  349.4 2.3 fusion.411
  357.6 2.2 fusion.426
  359.9 2.6 fusion.427
  362.5 2.3 fusion.429
  364.8 2.3 fusion.428
  369.3 2.6 fusion.424
  371.9 2.3 fusion.430
  374.2 2.3 fusion.425
  383.1 58.1 %psum.7 = f32[2,16,128]{2,1,0:T(8,128)S(1)} all-reduce(f32[2,16,128]{2,1,0:T(8,128)} %get-tuple-element.204), channel_id=1, replica_groups=mesh['tm'=16,'orb'=8] {'tm'}, use_global_device_ids=true, to_apply=%region_9.10 | all-reduce | flops 4096 | bytes 32768 | tf_op jit(solution)/shard_map/psum | solution.py:132
  441.1 28.1 %all_gather.7 = f32[2,128,128]{2,1,0:T(8,128)S(1)} all-gather(f32[2,16,128]{2,1,0:T(8,128)S(1)} %psum.7), channel_id=1, replica_groups=mesh['tm'=16,'orb'=8] {'orb'}, dimensions={1}, use_global_device_ids=true | all-gather | bytes 147456 | tf_op jit(solution)/shard_map/all_gather | solution.py:133
  (255 shorter events, 132.2 us)
Async XLA Ops:
  6.5 2.5 copy-start
  6.5 43.6 %all-gather.2.cloned.1.call-start = ((), (), s32[]{:S(2)}) async-start(), calls=%async_computation.1 | async-start | bytes 4718592 | tf_op jit(solution)/shard_map/all_gather | solution.py:126
  10.6 46.1 %copy-start.11 = (s32[512]{0:T(512)S(1)}, s32[512]{0:T(512)}, u32[]{:S(2)}) copy-start(s32[512]{0:T(512)} %param.11) | copy-start | bytes 6148
  50.1 69.5 %all-to-all-start = ((bf16[2,2,32,128,128]{4,3,1,0,2:T(8,128)(2,1)}), bf16[2,2,32,128,128]{4,3,1,0,2:T(8,128)(2,1)}, u32[]{:S(2)}, u32[]{:S(2)}) async-start(bf16[2,2,32,128,128]{4,3,1,0,2:T(8,128)(2,1)} %all-gather.2.cloned.1.call-done), calls=%async_computation | async-start | bytes 8388608 | tf_op jit(solution)/shard_map/all_to_all | solution.py:127
  57.9 1.1 copy-start.9
  58.0 1.2 copy-start.10
  58.0 3.1 copy-start.8
  134.1 0.5 copy-start.12
  134.1 6.7 %copy-start.2 = (bf16[128,128]{1,0:T(8,128)(2,1)}, bf16[128,128]{1,0:T(8,128)(2,1)S(1)}, u32[]{:S(2)}) copy-start(bf16[128,128]{1,0:T(8,128)(2,1)S(1)} %get-tuple-element.394) | copy-start | bytes 98308 | tf_op jit(solution)/shard_map/while
  160.4 4.5 copy-start.5
  185.2 4.5 copy-start.3
  185.2 4.5 copy-start.4
  187.5 8.3 %copy-start.6 = (f32[2,16,128]{2,1,0:T(8,128)S(1)}, f32[2,16,128]{2,1,0:T(8,128)}, u32[]{:S(2)}) copy-start(f32[2,16,128]{2,1,0:T(8,128)} %get-tuple-element.375) | copy-start | bytes 49156 | tf_op jit(solution)/shard_map/while
  187.5 8.9 %copy-start.13 = (f32[32]{0:T(128)S(1)}, f32[32]{0:T(128)}, u32[]{:S(2)}) copy-start(f32[32]{0:T(128)} %copy-done.12) | copy-start | bytes 388 | tf_op jit(solution)/shard_map/while
  195.7 0.6 copy-start.7
  196.4 0.5 copy-start.12
  196.4 6.7 %copy-start.2 = (bf16[128,128]{1,0:T(8,128)(2,1)}, bf16[128,128]{1,0:T(8,128)(2,1)S(1)}, u32[]{:S(2)}) copy-start(bf16[128,128]{1,0:T(8,128)(2,1)S(1)} %get-tuple-element.394) | copy-start | bytes 98308 | tf_op jit(solution)/shard_map/while
  222.7 4.5 copy-start.5
  247.4 4.5 copy-start.3
  247.4 4.5 copy-start.4
  249.7 8.3 %copy-start.6 = (f32[2,16,128]{2,1,0:T(8,128)S(1)}, f32[2,16,128]{2,1,0:T(8,128)}, u32[]{:S(2)}) copy-start(f32[2,16,128]{2,1,0:T(8,128)} %get-tuple-element.375) | copy-start | bytes 49156 | tf_op jit(solution)/shard_map/while
  249.7 8.9 %copy-start.13 = (f32[32]{0:T(128)S(1)}, f32[32]{0:T(128)}, u32[]{:S(2)}) copy-start(f32[32]{0:T(128)} %copy-done.12) | copy-start | bytes 388 | tf_op jit(solution)/shard_map/while
  258.0 0.6 copy-start.7
  258.6 0.5 copy-start.12
  258.6 6.7 %copy-start.2 = (bf16[128,128]{1,0:T(8,128)(2,1)}, bf16[128,128]{1,0:T(8,128)(2,1)S(1)}, u32[]{:S(2)}) copy-start(bf16[128,128]{1,0:T(8,128)(2,1)S(1)} %get-tuple-element.394) | copy-start | bytes 98308 | tf_op jit(solution)/shard_map/while
  284.9 4.5 copy-start.5
  309.7 4.5 copy-start.3
  309.7 4.5 copy-start.4
  311.9 8.3 %copy-start.6 = (f32[2,16,128]{2,1,0:T(8,128)S(1)}, f32[2,16,128]{2,1,0:T(8,128)}, u32[]{:S(2)}) copy-start(f32[2,16,128]{2,1,0:T(8,128)} %get-tuple-element.375) | copy-start | bytes 49156 | tf_op jit(solution)/shard_map/while
  311.9 8.9 %copy-start.13 = (f32[32]{0:T(128)S(1)}, f32[32]{0:T(128)}, u32[]{:S(2)}) copy-start(f32[32]{0:T(128)} %copy-done.12) | copy-start | bytes 388 | tf_op jit(solution)/shard_map/while
  320.2 0.6 copy-start.7
  320.8 0.5 copy-start.12
  320.8 6.7 %copy-start.2 = (bf16[128,128]{1,0:T(8,128)(2,1)}, bf16[128,128]{1,0:T(8,128)(2,1)S(1)}, u32[]{:S(2)}) copy-start(bf16[128,128]{1,0:T(8,128)(2,1)S(1)} %get-tuple-element.394) | copy-start | bytes 98308 | tf_op jit(solution)/shard_map/while
  347.1 4.5 copy-start.5
  371.9 4.5 copy-start.3
  371.9 4.5 copy-start.4
  374.2 8.3 %copy-start.6 = (f32[2,16,128]{2,1,0:T(8,128)S(1)}, f32[2,16,128]{2,1,0:T(8,128)}, u32[]{:S(2)}) copy-start(f32[2,16,128]{2,1,0:T(8,128)} %get-tuple-element.375) | copy-start | bytes 49156 | tf_op jit(solution)/shard_map/while
  374.2 8.9 %copy-start.13 = (f32[32]{0:T(128)S(1)}, f32[32]{0:T(128)}, u32[]{:S(2)}) copy-start(f32[32]{0:T(128)} %copy-done.12) | copy-start | bytes 388 | tf_op jit(solution)/shard_map/while
  382.5 0.6 copy-start.7
  383.1 89.1 %copy-start.1 = (bf16[2,2,32,16,128]{4,3,2,1,0:T(8,128)(2,1)S(1)}, bf16[2,2,32,16,128]{4,3,2,1,0:T(8,128)(2,1)}, u32[]{:S(2)}) copy-start(bf16[2,2,32,16,128]{4,3,2,1,0:T(8,128)(2,1)} %param.10) | copy-start | bytes 1572868
Sparse Core Ops, SparseCore 0:
  10.7 39.3 all-gather.1
where the time goes:
time: 482 us; the launch traced here: 479 us
  matrix products  219 us (45%)
  waiting for transfers between devices  95.1 us (20%)
  blocking collectives  86.2 us (18%)
  local copies, waits for them, and re-layouts  46.3 us (10%)
  between operations  13.6 us (3%)
  other arithmetic  11.6 us (2%)
  starting transfers between devices  6.58 us (1%)
    psum x1, blocking collectives, on_device(): summed_rows = lax.psum(local_collision, 'tm')  58.1 us
    all_to_all x1, waiting for transfers between devices, on_device(): lax.all_to_all(full_sorted, 'tm', split_axis=2, concat_axis=2, tiled=True)  55.6 us
    dot_general x24, matrix products, complex_einsum(): jnp.einsum(form, left_re, right_im, preferred_element_type=jnp.float32)  48.3 us
    dot_general x24, matrix products, complex_einsum(): jnp.einsum(form, left_im, right_im, preferred_element_type=jnp.float32)  48.2 us
    dot_general x24, matrix products, complex_einsum(): jnp.einsum(form, left_im, right_re, preferred_element_type=jnp.float32)  45 us
    dot_general x24, matrix products, complex_einsum(): jnp.einsum(form, left_re, right_re, preferred_element_type=jnp.float32)  44.8 us
    all_gather x1, waiting for transfers between devices, on_device(): full_sorted = lax.all_gather(sorted_slab, 'orb', axis=3, tiled=True)  39.5 us
    all_gather x1, blocking collectives, on_device(): collision = lax.all_gather(summed_rows, 'orb', axis=1, tiled=True)  28.1 us
  transfers between devices with their start and end apart: 2, of which 2 were waited for; matrix products, arithmetic and copies ran while one was open for 1% of the time, Pallas kernels for 0%

commit v1 on v0

--- a/solution.py
+++ b/solution.py
@@ -3,6 +3,7 @@
 import jax.numpy as jnp
 from jax import lax
 from jax.sharding import PartitionSpec as P
+from jax.lax import all_gather
 
 history_step = 0.02
 update_step = 0.5
@@ -129,7 +130,12 @@
     local_collision = history_terms(
         forward, back_full, weights, interaction, inter_rows, row_start, row_count
     )
-    summed_rows = lax.psum(local_collision, "tm")
+
+    def lift_strips_all(block_here, net_axis):
+        aux = all_gather(block_here, axis_name=net_axis).sum(axis=0)
+        return aux
+
+    summed_rows = lift_strips_all(local_collision, "tm")
     collision = lax.all_gather(summed_rows, "orb", axis=1, tiled=True)
     own_rows = lax.dynamic_slice_in_dim(collision, row_start, row_count, 1)
     own_columns = lax.dynamic_slice_in_dim(collision, row_start, row_count, 2)

time: 482 us -> 433 us (0.90)
  blocking collectives: 86.2 us -> 36.8 us
    psum x1 -> x0, blocking collectives: 58.1 us -> none  [on_device(): summed_rows = lax.psum(local_collision, 'tm')]
    all_gather x0 -> x1, blocking collectives: none -> 17.6 us  [lift_strips_all(): aux = all_gather(block_here, axis_name=net_axis).sum(axis=0)]
    all_gather x1, blocking collectives: 28.1 us -> 19.2 us  [on_device(): collision = lax.all_gather(summed_rows, 'orb', axis=1, tiled=True)]
  transfers between devices with their start and end apart: 2 -> 2, of which waited for: 2 -> 2; matrix products, arithmetic and copies ran while one was open for 1% -> 2% of each run, Pallas kernels for 0% -> 0%
where the time goes in v1:
time: 433 us; the launch traced here: 430 us
  matrix products  219 us (51%)
  waiting for transfers between devices  95.1 us (22%)
  local copies, waits for them, and re-layouts  46.3 us (11%)
  blocking collectives  36.8 us (8%)
  between operations  13.6 us (3%)
  other arithmetic  11.6 us (3%)
  starting transfers between devices  6.58 us (2%)
    all_to_all x1, waiting for transfers between devices, on_device(): lax.all_to_all(full_sorted, 'tm', split_axis=2, concat_axis=2, tiled=True)  55.6 us
    dot_general x24, matrix products, complex_einsum(): jnp.einsum(form, left_re, right_im, preferred_element_type=jnp.float32)  48.3 us
    dot_general x24, matrix products, complex_einsum(): jnp.einsum(form, left_im, right_im, preferred_element_type=jnp.float32)  48.2 us
    dot_general x24, matrix products, complex_einsum(): jnp.einsum(form, left_im, right_re, preferred_element_type=jnp.float32)  45 us
    dot_general x24, matrix products, complex_einsum(): jnp.einsum(form, left_re, right_re, preferred_element_type=jnp.float32)  44.8 us
    all_gather x1, waiting for transfers between devices, on_device(): full_sorted = lax.all_gather(sorted_slab, 'orb', axis=3, tiled=True)  39.5 us
    all_gather x1, blocking collectives, on_device(): collision = lax.all_gather(summed_rows, 'orb', axis=1, tiled=True)  19.2 us
    all_gather x1, blocking collectives, lift_strips_all(): aux = all_gather(block_here, axis_name=net_axis).sum(axis=0)  17.6 us
  transfers between devices with their start and end apart: 2, of which 2 were waited for; matrix products, arithmetic and copies ran while one was open for 2% of the time, Pallas kernels for 0%

profile of v1, /device:TPU:1, one launch (start us, length us, event | category | flops | bytes accessed | tf_op | source)
XLA Modules:
  0.0 429.7 jit_solution(7471554814628150537)
XLA Ops:
  10.6 39.5 %all-gather.3.cloned.1.call-done = bf16[2,2,32,128,128]{4,3,1,0,2:T(8,128)(2,1)} async-done(((bf16[2,2,32,16,128]{4,3,1,0,2:T(8,128)(2,1)}), bf16[2,2,32,128,128]{4,3,1,0,2:T(8,128)(2,1)}) %all-gather.3.cloned.1.call-update) | async-done | bytes 4194320 | tf_op jit(solution)/shard_map/all_gather | solution.py:127
  50.1 6.6 %all-to-all-start = ((bf16[2,2,32,128,128]{4,3,1,0,2:T(8,128)(2,1)}), bf16[2,2,32,128,128]{4,3,1,0,2:T(8,128)(2,1)}, u32[]{:S(2)}, u32[]{:S(2)}) async-start(bf16[2,2,32,128,128]{4,3,1,0,2:T(8,128)(2,1)} %all-gather.3.cloned.1.call-done), calls=%async_computation | async-start | bytes 8388608 | tf_op jit(solution)/shard_map/all_to_all | solution.py:128
  64.0 55.6 %all-to-all-done = bf16[2,2,32,128,128]{4,3,1,0,2:T(8,128)(2,1)} async-done(((bf16[2,2,32,128,128]{4,3,1,0,2:T(8,128)(2,1)}), bf16[2,2,32,128,128]{4,3,1,0,2:T(8,128)(2,1)}, u32[]{:S(2)}, u32[]{:S(2)}) %all-to-all-start) | async-done | bytes 4194336 | tf_op jit(solution)/shard_map/all_to_all | solution.py:128
  119.6 4.7 %copy.65 = bf16[2,2,32,128,128]{4,3,2,1,0:T(8,128)(2,1)} copy(bf16[2,2,32,128,128]{4,3,1,0,2:T(8,128)(2,1)} %all-to-all-done) | data formatting | bytes 8388608 | tf_op jit(solution)/shard_map/all_to_all | solution.py:128
  124.3 5.2 %gather_fusion.1 = bf16[32,2,2,128,128]{4,3,2,1,0:T(8,128)(2,1)} fusion(bf16[2,2,32,128,128]{4,3,2,1,0:T(8,128)(2,1)} %copy.65, s32[1024]{0:T(1024)S(1)} %pad_clamp_fusion), kind=kCustom, calls=%fused_computation.1 | custom fusion | bytes 8388736 | tf_op jit(solution)/shard_map/jit(_take)/gather | solution.py:129
  129.5 4.6 %select_bitcast_fusion = bf16[2,2,32,128,128]{4,3,1,0,2:T(8,128)(2,1)} fusion(bf16[32,2,2,128,128]{4,3,2,1,0:T(8,128)(2,1)} %gather_fusion.1, pred[32]{0:T(512)(128)(4,1)S(1)} %compare_and_fusion.1), kind=kLoop, calls=%fused_computation.226 | loop fusion | flops 2097152 | bytes 8388640 | tf_op jit(solution)/shard_map/jit(_take)/select_n | solution.py:129
  134.1 249.0 %while.16 = (s32[]{:T(128)}, f32[2,16,128]{2,1,0:T(8,128)}, f32[32]{0:T(128)S(1)}, bf16[2,2,32,128,128]{4,3,2,1,0:T(8,128)(2,1)}, s32[]{:T(128)}, /*index=5*/bf1...) while((s32[]{:T(128)}, f32[2,16,128]{2,1,0:T(8,128)}, ...), condition=%wide.region_8.9_spmd.clone, body=%wide.region_3.8_spmd.clone.sunk | while | flops 4459808768 | bytes 142112496 | solution.py:98
  148.4 2.6 fusion.413
  151.0 2.3 fusion.415
  153.3 2.3 fusion.414
  155.6 2.2 fusion.409
  157.8 2.6 fusion.410
  160.4 2.3 fusion.416
  162.7 2.3 fusion.411
  170.9 2.2 fusion.426
  173.2 2.6 fusion.427
  175.8 2.3 fusion.429
  178.1 2.3 fusion.428
  180.3 2.2 fusion.423
  182.5 2.6 fusion.424
  185.2 2.3 fusion.430
  187.5 2.3 fusion.425
  210.6 2.6 fusion.413
  213.3 2.3 fusion.415
  215.5 2.3 fusion.414
  217.8 2.2 fusion.409
  220.0 2.6 fusion.410
  222.7 2.3 fusion.416
  224.9 2.3 fusion.411
  233.2 2.2 fusion.426
  235.4 2.6 fusion.427
  238.0 2.3 fusion.429
  240.3 2.3 fusion.428
  244.8 2.6 fusion.424
  247.4 2.3 fusion.430
  249.7 2.3 fusion.425
  272.9 2.6 fusion.413
  275.5 2.3 fusion.415
  277.8 2.3 fusion.414
  282.3 2.6 fusion.410
  284.9 2.3 fusion.416
  287.2 2.3 fusion.411
  295.4 2.2 fusion.426
  297.6 2.6 fusion.427
  300.3 2.3 fusion.429
  302.5 2.3 fusion.428
  307.0 2.6 fusion.424
  309.7 2.3 fusion.430
  311.9 2.3 fusion.425
  335.1 2.6 fusion.413
  337.8 2.3 fusion.415
  340.0 2.3 fusion.414
  344.5 2.6 fusion.410
  347.2 2.3 fusion.416
  349.4 2.3 fusion.411
  357.6 2.2 fusion.426
  359.9 2.6 fusion.427
  362.5 2.3 fusion.429
  364.8 2.3 fusion.428
  369.3 2.6 fusion.424
  371.9 2.3 fusion.430
  374.2 2.3 fusion.425
  383.1 17.6 %all-gather = f32[32,16,128]{2,1,0:T(8,128)S(1)} all-gather(f32[2,16,128]{2,1,0:T(8,128)} %get-tuple-element.204), channel_id=2, replica_groups=mesh['tm'=16,'orb'=8] {'tm'}, dimensions={0}, use_global_device_ids=true | all-gather | bytes 278528 | tf_op jit(solution)/shard_map/all_gather | solution.py:135
  400.7 19.2 %all_gather.15 = f32[2,128,128]{2,1,0:T(8,128)S(1)} all-gather(f32[2,16,128]{2,1,0:T(8,128)S(1)} %reduce_sum.69), channel_id=1, replica_groups=mesh['tm'=16,'orb'=8] {'orb'}, dimensions={1}, use_global_device_ids=true | all-gather | bytes 147456 | tf_op jit(solution)/shard_map/all_gather | solution.py:139
  (256 shorter events, 132.2 us)
Async XLA Ops:
  6.5 2.5 copy-start
  6.5 43.6 %all-gather.3.cloned.1.call-start = ((), (), s32[]{:S(2)}) async-start(), calls=%async_computation.1 | async-start | bytes 4718592 | tf_op jit(solution)/shard_map/all_gather | solution.py:127
  10.6 46.1 %copy-start.11 = (s32[512]{0:T(512)S(1)}, s32[512]{0:T(512)}, u32[]{:S(2)}) copy-start(s32[512]{0:T(512)} %param.11) | copy-start | bytes 6148
  50.1 69.5 %all-to-all-start = ((bf16[2,2,32,128,128]{4,3,1,0,2:T(8,128)(2,1)}), bf16[2,2,32,128,128]{4,3,1,0,2:T(8,128)(2,1)}, u32[]{:S(2)}, u32[]{:S(2)}) async-start(bf16[2,2,32,128,128]{4,3,1,0,2:T(8,128)(2,1)} %all-gather.3.cloned.1.call-done), calls=%async_computation | async-start | bytes 8388608 | tf_op jit(solution)/shard_map/all_to_all | solution.py:128
  57.9 1.1 copy-start.9
  58.0 1.2 copy-start.10
  58.0 3.1 copy-start.8
  134.1 0.5 copy-start.12
  134.1 6.7 %copy-start.2 = (bf16[128,128]{1,0:T(8,128)(2,1)}, bf16[128,128]{1,0:T(8,128)(2,1)S(1)}, u32[]{:S(2)}) copy-start(bf16[128,128]{1,0:T(8,128)(2,1)S(1)} %get-tuple-element.402) | copy-start | bytes 98308 | tf_op jit(solution)/shard_map/while
  160.4 4.5 %copy-start.5 = (f32[8,16,128]{2,1,0:T(8,128)S(1)}, f32[8,16,128]{2,1,0:T(8,128)}, u32[]{:S(2)}) copy-start(f32[8,16,128]{2,1,0:T(8,128)} %fusion.408) | copy-start | bytes 196612 | tf_op jit(solution)/shard_map/while
  185.2 4.5 %copy-start.3 = (bf16[128,128]{1,0:T(8,128)(2,1)S(1)}, bf16[128,128]{1,0:T(8,128)(2,1)}, u32[]{:S(2)}) copy-start(bf16[128,128]{1,0:T(8,128)(2,1)} %copy-done.2) | copy-start | bytes 98308 | tf_op jit(solution)/shard_map/while
  185.2 4.5 %copy-start.4 = (f32[8,16,128]{2,1,0:T(8,128)S(1)}, f32[8,16,128]{2,1,0:T(8,128)}, u32[]{:S(2)}) copy-start(f32[8,16,128]{2,1,0:T(8,128)} %fusion.422) | copy-start | bytes 196612 | tf_op jit(solution)/shard_map/while
  187.5 8.3 %copy-start.6 = (f32[2,16,128]{2,1,0:T(8,128)S(1)}, f32[2,16,128]{2,1,0:T(8,128)}, u32[]{:S(2)}) copy-start(f32[2,16,128]{2,1,0:T(8,128)} %get-tuple-element.383) | copy-start | bytes 49156 | tf_op jit(solution)/shard_map/while
  187.5 8.9 %copy-start.13 = (f32[32]{0:T(128)S(1)}, f32[32]{0:T(128)}, u32[]{:S(2)}) copy-start(f32[32]{0:T(128)} %copy-done.12) | copy-start | bytes 388 | tf_op jit(solution)/shard_map/while
  195.7 0.6 copy-start.7
  196.4 0.5 copy-start.12
  196.4 6.7 %copy-start.2 = (bf16[128,128]{1,0:T(8,128)(2,1)}, bf16[128,128]{1,0:T(8,128)(2,1)S(1)}, u32[]{:S(2)}) copy-start(bf16[128,128]{1,0:T(8,128)(2,1)S(1)} %get-tuple-element.402) | copy-start | bytes 98308 | tf_op jit(solution)/shard_map/while
  222.7 4.5 %copy-start.5 = (f32[8,16,128]{2,1,0:T(8,128)S(1)}, f32[8,16,128]{2,1,0:T(8,128)}, u32[]{:S(2)}) copy-start(f32[8,16,128]{2,1,0:T(8,128)} %fusion.408) | copy-start | bytes 196612 | tf_op jit(solution)/shard_map/while
  247.4 4.5 %copy-start.3 = (bf16[128,128]{1,0:T(8,128)(2,1)S(1)}, bf16[128,128]{1,0:T(8,128)(2,1)}, u32[]{:S(2)}) copy-start(bf16[128,128]{1,0:T(8,128)(2,1)} %copy-done.2) | copy-start | bytes 98308 | tf_op jit(solution)/shard_map/while
  247.4 4.5 %copy-start.4 = (f32[8,16,128]{2,1,0:T(8,128)S(1)}, f32[8,16,128]{2,1,0:T(8,128)}, u32[]{:S(2)}) copy-start(f32[8,16,128]{2,1,0:T(8,128)} %fusion.422) | copy-start | bytes 196612 | tf_op jit(solution)/shard_map/while
  249.7 8.3 %copy-start.6 = (f32[2,16,128]{2,1,0:T(8,128)S(1)}, f32[2,16,128]{2,1,0:T(8,128)}, u32[]{:S(2)}) copy-start(f32[2,16,128]{2,1,0:T(8,128)} %get-tuple-element.383) | copy-start | bytes 49156 | tf_op jit(solution)/shard_map/while
  249.7 8.9 %copy-start.13 = (f32[32]{0:T(128)S(1)}, f32[32]{0:T(128)}, u32[]{:S(2)}) copy-start(f32[32]{0:T(128)} %copy-done.12) | copy-start | bytes 388 | tf_op jit(solution)/shard_map/while
  258.0 0.6 copy-start.7
  258.6 0.5 copy-start.12
  258.6 6.7 %copy-start.2 = (bf16[128,128]{1,0:T(8,128)(2,1)}, bf16[128,128]{1,0:T(8,128)(2,1)S(1)}, u32[]{:S(2)}) copy-start(bf16[128,128]{1,0:T(8,128)(2,1)S(1)} %get-tuple-element.402) | copy-start | bytes 98308 | tf_op jit(solution)/shard_map/while
  284.9 4.5 %copy-start.5 = (f32[8,16,128]{2,1,0:T(8,128)S(1)}, f32[8,16,128]{2,1,0:T(8,128)}, u32[]{:S(2)}) copy-start(f32[8,16,128]{2,1,0:T(8,128)} %fusion.408) | copy-start | bytes 196612 | tf_op jit(solution)/shard_map/while
  309.7 4.5 %copy-start.3 = (bf16[128,128]{1,0:T(8,128)(2,1)S(1)}, bf16[128,128]{1,0:T(8,128)(2,1)}, u32[]{:S(2)}) copy-start(bf16[128,128]{1,0:T(8,128)(2,1)} %copy-done.2) | copy-start | bytes 98308 | tf_op jit(solution)/shard_map/while
  309.7 4.5 %copy-start.4 = (f32[8,16,128]{2,1,0:T(8,128)S(1)}, f32[8,16,128]{2,1,0:T(8,128)}, u32[]{:S(2)}) copy-start(f32[8,16,128]{2,1,0:T(8,128)} %fusion.422) | copy-start | bytes 196612 | tf_op jit(solution)/shard_map/while
  311.9 8.3 %copy-start.6 = (f32[2,16,128]{2,1,0:T(8,128)S(1)}, f32[2,16,128]{2,1,0:T(8,128)}, u32[]{:S(2)}) copy-start(f32[2,16,128]{2,1,0:T(8,128)} %get-tuple-element.383) | copy-start | bytes 49156 | tf_op jit(solution)/shard_map/while
  311.9 8.9 %copy-start.13 = (f32[32]{0:T(128)S(1)}, f32[32]{0:T(128)}, u32[]{:S(2)}) copy-start(f32[32]{0:T(128)} %copy-done.12) | copy-start | bytes 388 | tf_op jit(solution)/shard_map/while
  320.2 0.6 copy-start.7
  320.8 0.5 copy-start.12
  320.8 6.7 %copy-start.2 = (bf16[128,128]{1,0:T(8,128)(2,1)}, bf16[128,128]{1,0:T(8,128)(2,1)S(1)}, u32[]{:S(2)}) copy-start(bf16[128,128]{1,0:T(8,128)(2,1)S(1)} %get-tuple-element.402) | copy-start | bytes 98308 | tf_op jit(solution)/shard_map/while
  347.1 4.5 %copy-start.5 = (f32[8,16,128]{2,1,0:T(8,128)S(1)}, f32[8,16,128]{2,1,0:T(8,128)}, u32[]{:S(2)}) copy-start(f32[8,16,128]{2,1,0:T(8,128)} %fusion.408) | copy-start | bytes 196612 | tf_op jit(solution)/shard_map/while
  371.9 4.5 %copy-start.3 = (bf16[128,128]{1,0:T(8,128)(2,1)S(1)}, bf16[128,128]{1,0:T(8,128)(2,1)}, u32[]{:S(2)}) copy-start(bf16[128,128]{1,0:T(8,128)(2,1)} %copy-done.2) | copy-start | bytes 98308 | tf_op jit(solution)/shard_map/while
  371.9 4.5 %copy-start.4 = (f32[8,16,128]{2,1,0:T(8,128)S(1)}, f32[8,16,128]{2,1,0:T(8,128)}, u32[]{:S(2)}) copy-start(f32[8,16,128]{2,1,0:T(8,128)} %fusion.422) | copy-start | bytes 196612 | tf_op jit(solution)/shard_map/while
  374.2 8.3 %copy-start.6 = (f32[2,16,128]{2,1,0:T(8,128)S(1)}, f32[2,16,128]{2,1,0:T(8,128)}, u32[]{:S(2)}) copy-start(f32[2,16,128]{2,1,0:T(8,128)} %get-tuple-element.383) | copy-start | bytes 49156 | tf_op jit(solution)/shard_map/while
  374.2 8.9 %copy-start.13 = (f32[32]{0:T(128)S(1)}, f32[32]{0:T(128)}, u32[]{:S(2)}) copy-start(f32[32]{0:T(128)} %copy-done.12) | copy-start | bytes 388 | tf_op jit(solution)/shard_map/while
  382.5 0.6 copy-start.7
  383.1 39.8 %copy-start.1 = (bf16[2,2,32,16,128]{4,3,2,1,0:T(8,128)(2,1)S(1)}, bf16[2,2,32,16,128]{4,3,2,1,0:T(8,128)(2,1)}, u32[]{:S(2)}) copy-start(bf16[2,2,32,16,128]{4,3,2,1,0:T(8,128)(2,1)} %param.10) | copy-start | bytes 1572868
Sparse Core Ops, SparseCore 0:
  10.7 39.3 all-gather.2
